TPU v7x, 256 devices: a whole 4x4x8 slice. The times are simulated.
256 devices in a mesh: sub: 64 (over x, z, core), slab: 4 (over y).
Axes of the slice: x: 4, y: 4, z: 8, core: 2. Of those that a mesh axis runs over, the one named last changes fastest.
Arguments:
- adjoint_load: float32 [4, 64, 2, 4, 3200], P('slab', 'sub')
- design: float32 [4, 64, 2032], P('slab', 'sub'), may hold values from 0 to 1
- viscous_block: float32 [24, 24], replicated
- brinkman_block: float32 [24, 24], replicated
- coupling: float32 [8, 24], replicated, may hold values from -1.2 to 1.2
- stabilization: float32 [8, 8], replicated
- neighbours: int32 [4, 64, 3], P('slab', 'sub'), may hold values from -1 to 63, as said below
- iface_nodes: int32 [4, 64, 3, 256], P('slab', 'sub'), may hold values from 0 to 3199, as said below
- iface_count: int32 [4, 64, 3], P('slab', 'sub'), may hold values from 0 to 256, as said below
- face_nodes: int32 [4, 64, 2, 512], P('slab', 'sub'), may hold values from 0 to 3199, as said below
- owner_ids: int32 [4, 64, 3, 256], P('slab', 'sub'), may hold values from 0 to 63, as said below
Outputs:
- solution: float32 [4, 64, 2, 4, 3200], P('slab', 'sub')
- coefficients: float32 [2, 3], replicated
Inputs may be any that keep to these rules, and one draw needn't show every extreme that they name: In round r the neighbour of subdomain i is i XOR 2^r or -1 for none; two neighbours list each other. `iface_nodes`: per subdomain, all entries here and in face_nodes are distinct local nodes. Slot k of round r names the same physical node on a subdomain and on its round-r neighbour; only the first iface_count slots are shared. `iface_count`: equal on both sides of a pair, 0 where the round has no neighbour. `face_nodes`: face 0 is the lower face, face 1 the upper one; slot k of the upper face of slab s is slot k of the lower face of slab s + 1 at the same index along sub. `owner_ids`: for a used slot, one of the two subdomains of the pair, the same on both sides; for an unused slot, the subdomain's own index.
All inputs are finite; a program needn't handle non-finite values.
Results may differ from a plain program's by a relative error of at most 0.0003.
Values sent between devices are 32-bit elements; how exact they have to be, the bound alone decides.
No kernel may reach another device: no remote copies, remote signals or barrier semaphores. Data moves between devices by JAX's collectives and lax.ppermute only.
A program may use at most 128 MiB of HBM per device.

v0:
```python
import jax
import jax.numpy as jnp
from jax import lax
from jax.sharding import PartitionSpec as P

EX = 4
EY = 4
EZ = 127
IFACE = 256
ROUNDS = 3
KRYLOV = 3
CASES = 2
ELEMS = 2032
NODES = 3200
PRECISE = lax.Precision.HIGHEST
BRINKMAN_MAX = 4.0
RAMP_PARAM = 0.1


def swapped(block, axis, bit):
    count = lax.axis_size(axis)
    route = []
    for low in range(count):
        high = low | 1 << bit
        if high != low and high < count:
            route += [(low, high), (high, low)]
    return lax.ppermute(block, axis, route)


def extended_2(block, sides, width):
    for axis, dim in sides:
        count = lax.axis_size(axis)
        forward = [(i, i + 1) for i in range(count - 1)]
        backward = [(target, source) for source, target in forward]
        low = lax.ppermute(
            lax.slice_in_dim(block, block.shape[dim] - width, None, axis=dim), axis, forward
        )
        high = lax.ppermute(lax.slice_in_dim(block, 0, width, axis=dim), axis, backward)
        block = jnp.concatenate([low, block, high], axis=dim)
    return block


def corner_offsets(corner):
    return (corner // 4, corner // 2 % 2, corner % 2)


def element_vectors(field):
    channels = field.shape[0]
    node_grid = field.reshape(channels, EX + 1, EY + 1, EZ + 1)
    corner_list = []
    for corner in range(8):
        shift_x, shift_y, shift_z = corner_offsets(corner)
        window = node_grid[
            :, shift_x : shift_x + EX, shift_y : shift_y + EY, shift_z : shift_z + EZ
        ]
        corner_list.append(window.reshape(channels, ELEMS))
    return jnp.stack(corner_list, axis=1)


def node_sums(element_out):
    channels = element_out.shape[0]
    summed = jnp.zeros((channels, EX + 1, EY + 1, EZ + 1), jnp.float32)
    for corner in range(8):
        shift_x, shift_y, shift_z = corner_offsets(corner)
        corner_block = element_out[:, corner].reshape(channels, EX, EY, EZ)
        summed = summed + jnp.pad(
            corner_block,
            ((0, 0), (shift_x, 1 - shift_x), (shift_y, 1 - shift_y), (shift_z, 1 - shift_z)),
        )
    return summed.reshape(channels, NODES)


def brinkman_of(design):
    return BRINKMAN_MAX * RAMP_PARAM * (1.0 - design) / (RAMP_PARAM + design)


def adjoint_terms(state, brinkman, viscous_block, brinkman_block, coupling, stabilization):
    values = element_vectors(state).reshape(CASES, 32, ELEMS)
    velocity = values[:, :24]
    pressure = values[:, 24:]
    out_velocity = jnp.einsum("ij,cie->cje", viscous_block, velocity, precision=PRECISE)
    out_velocity = out_velocity + brinkman * jnp.einsum(
        "ij,cie->cje", brinkman_block, velocity, precision=PRECISE
    )
    out_velocity = out_velocity + jnp.einsum("kj,cke->cje", coupling, pressure, precision=PRECISE)
    out_pressure = jnp.einsum("kj,cje->cke", coupling, velocity, precision=PRECISE) - jnp.einsum(
        "lk,cle->cke", stabilization, pressure, precision=PRECISE
    )
    element_out = jnp.concatenate([out_velocity, out_pressure], axis=1).reshape(CASES * 4, 8, ELEMS)
    return node_sums(element_out)


def divergence_terms(velocity_nodes, coupling):
    element_vel = element_vectors(velocity_nodes).reshape(CASES, 24, ELEMS)
    return node_sums(jnp.einsum("kj,cje->cke", coupling, element_vel, precision=PRECISE))


def gradient_terms(pressure_nodes, coupling):
    element_pre = element_vectors(pressure_nodes)
    element_out = jnp.einsum("kj,cke->cje", coupling, element_pre, precision=PRECISE).reshape(
        CASES * 3, 8, ELEMS
    )
    return node_sums(element_out)


def diagonal_terms(brinkman, viscous_block, brinkman_block):
    diag_elem = (
        jnp.diagonal(viscous_block)[:, None]
        + jnp.diagonal(brinkman_block)[:, None] * brinkman[None, :]
    )
    return node_sums(diag_elem.reshape(3, 8, ELEMS))


def schur_terms(diag_nodes, coupling, stabilization):
    inverse = 1.0 / element_vectors(diag_nodes).reshape(24, ELEMS)
    schur_elem = (
        jnp.einsum("kj,je->ke", coupling * coupling, inverse, precision=PRECISE)
        + jnp.diagonal(stabilization)[:, None]
    )
    return node_sums(schur_elem[None])


def node_weights(iface_nodes, not_owned, lower_face, lower_lost):
    weights = jnp.ones((NODES,), jnp.float32)
    for matching in range(ROUNDS):
        keep = jnp.where(not_owned[matching], 0.0, 1.0).astype(weights.dtype)
        weights = weights.at[iface_nodes[matching]].multiply(keep)
    return weights.at[lower_face].multiply(jnp.where(lower_lost, 0.0, 1.0).astype(weights.dtype))


def assemble(partial_sums, layout):
    iface_nodes, iface_count, neighbours, face_nodes = layout
    slot_ids = jnp.arange(IFACE, dtype=jnp.int32)
    slot_valid = (slot_ids[None, :] < iface_count[:, None]).astype(jnp.float32)
    outgoing = jnp.stack(
        [
            partial_sums[:, iface_nodes[matching]] * slot_valid[matching][None, :]
            for matching in range(ROUNDS)
        ]
    )
    present = (neighbours >= 0).astype(jnp.float32)
    incoming = jnp.stack(
        [swapped(outgoing[matching], "sub", matching) for matching in range(ROUNDS)]
    )
    incoming = incoming * present[:, None, None]
    face_out = jnp.stack([partial_sums[:, face_nodes[0]], partial_sums[:, face_nodes[1]]])
    extended = extended_2(face_out, (("slab", 0),), 1)
    summed = partial_sums
    for matching in range(ROUNDS):
        summed = summed.at[:, iface_nodes[matching]].add(incoming[matching])
    summed = summed.at[:, face_nodes[0]].add(extended[0])
    return summed.at[:, face_nodes[1]].add(extended[3])


def weighted_norms(vectors, weights):
    return lax.psum(jnp.sum(weights * vectors * vectors, axis=(1, 2)), ("sub", "slab"))


def triangular_solves(factor, target):
    middle = []
    for row_index in range(KRYLOV):
        remainder = target[:, row_index] - sum(
            (factor[:, row_index, col_index] * middle[col_index] for col_index in range(row_index))
        )
        middle.append(remainder / factor[:, row_index, row_index])
    result = [None] * KRYLOV
    for row_index in reversed(range(KRYLOV)):
        remainder = middle[row_index] - sum(
            (
                factor[:, col_index, row_index] * result[col_index]
                for col_index in range(row_index + 1, KRYLOV)
            )
        )
        result[row_index] = remainder / factor[:, row_index, row_index]
    return jnp.stack(result, axis=1)


def per_device(
    adjoint_load,
    design,
    viscous_block,
    brinkman_block,
    coupling,
    stabilization,
    neighbours,
    iface_nodes,
    iface_count,
    face_nodes,
    owner_ids,
):
    layout = (iface_nodes[0, 0], iface_count[0, 0], neighbours[0, 0], face_nodes[0, 0])
    brinkman = brinkman_of(design[0, 0])
    sub_index = lax.axis_index("sub")
    slab_index = lax.axis_index("slab")
    slot_ids = jnp.arange(IFACE, dtype=jnp.int32)
    not_owned = (slot_ids[None, :] < iface_count[0, 0][:, None]) & (owner_ids[0, 0] != sub_index)
    weights = node_weights(iface_nodes[0, 0], not_owned, face_nodes[0, 0, 0], slab_index > 0)
    owned_load = (adjoint_load[0, 0] * weights).reshape(CASES * 4, NODES)
    assembled = assemble(
        jnp.concatenate(
            [owned_load, diagonal_terms(brinkman, viscous_block, brinkman_block)], axis=0
        ),
        layout,
    )
    start_vec = assembled[: CASES * 4].reshape(CASES, 4, NODES)
    diag_nodes = assembled[CASES * 4 :]
    schur_diag = assemble(schur_terms(diag_nodes, coupling, stabilization), layout)[0]
    start_norm = jnp.sqrt(weighted_norms(start_vec, weights))
    krylov_basis = [start_vec / start_norm[:, None, None]]
    hessenberg = jnp.zeros((CASES, KRYLOV + 1, KRYLOV), jnp.float32)
    directions = []
    for krylov_step in range(KRYLOV):
        precondition_vector = krylov_basis[-1]
        velocity_guess = precondition_vector[:, :3] / diag_nodes[None]
        divergence = assemble(
            divergence_terms(velocity_guess.reshape(CASES * 3, NODES), coupling), layout
        )
        pressure = (divergence - precondition_vector[:, 3]) / schur_diag[None]
        gradient = assemble(gradient_terms(pressure, coupling), layout).reshape(CASES, 3, NODES)
        velocity = velocity_guess - gradient / diag_nodes[None]
        direction = jnp.concatenate([velocity, pressure[:, None]], axis=1)
        directions.append(direction)
        image_part = adjoint_terms(
            direction.reshape(CASES * 4, NODES),
            brinkman,
            viscous_block,
            brinkman_block,
            coupling,
            stabilization,
        )
        product_vec = assemble(image_part, layout).reshape(CASES, 4, NODES)
        local_heights = jnp.stack(
            [jnp.sum(weights * vector * product_vec, axis=(1, 2)) for vector in krylov_basis],
            axis=1,
        )
        heights = lax.psum(local_heights, ("sub", "slab"))
        for basis_index in range(len(krylov_basis)):
            product_vec = (
                product_vec - heights[:, basis_index, None, None] * krylov_basis[basis_index]
            )
        length = jnp.sqrt(weighted_norms(product_vec, weights))
        hessenberg = hessenberg.at[:, : krylov_step + 1, krylov_step].set(heights)
        hessenberg = hessenberg.at[:, krylov_step + 1, krylov_step].set(length)
        krylov_basis.append(product_vec / length[:, None, None])
    normal_matrix = jnp.einsum("cij,cik->cjk", hessenberg, hessenberg, precision=PRECISE)
    target = start_norm[:, None] * hessenberg[:, 0, :]
    factor = jnp.linalg.cholesky(normal_matrix)
    coefficients = triangular_solves(factor, target)
    solution = sum(
        (
            coefficients[:, krylov_step, None, None] * directions[krylov_step]
            for krylov_step in range(KRYLOV)
        )
    )
    return (solution[None, None], coefficients)


def solution(mesh):
    placed = (
        P("slab", "sub", None, None, None),
        P("slab", "sub", None),
        P(),
        P(),
        P(),
        P(),
        P("slab", "sub", None),
        P("slab", "sub", None, None),
        P("slab", "sub", None),
        P("slab", "sub", None, None),
        P("slab", "sub", None, None),
    )
    return jax.shard_map(
        per_device,
        mesh=mesh,
        in_specs=placed,
        out_specs=(P("slab", "sub", None, None, None), P()),
        check_vma=False,
    )
```

profile of v0, /device:TPU:1, one launch (start us, length us, event | category | flops | bytes accessed | tf_op | source)
XLA Modules:
  0.0 1081.2 jit_solution(7967894446121106461)
XLA Ops:
  12.2 3.3 scatter_fusion.2
  17.0 3.9 collective-permute-start.2
  27.3 3.2 collective-permute-start.3
  42.8 3.9 scatter_custom_fusion.7
  46.8 3.9 scatter_custom_fusion.8
  52.0 79.0 %psum.49 = f32[2]{0:T(128)S(1)} all-reduce(f32[2]{0:T(128)S(1)} %reduce_sum.120), channel_id=1, replica_groups=mesh['sub'=64,'slab'=4] {'sub','slab'}, use_global_device_ids=true, to_apply=%region_11.12 | all-reduce | flops 2 | bytes 16 | tf_op jit(solution)/shard_map/psum | solution.py:156
  143.9 3.3 fusion.120
  165.8 3.1 gather_fusion.16
  169.0 3.1 gather_fusion.17
  190.8 4.0 collective-permute-start.13
  204.5 3.3 scatter_fusion.9
  207.9 3.3 scatter_fusion.10
  211.3 4.1 scatter_custom_fusion.12
  215.4 3.9 scatter_custom_fusion.13
  234.2 4.0 pad_add_fusion.5
  247.5 4.3 collective-permute-start.18
  261.6 4.0 scatter_custom_fusion.22
  265.7 4.2 scatter_custom_fusion.23
  288.6 4.0 pad_add_fusion.4
  302.9 4.3 collective-permute-start.23
  317.1 4.0 scatter_custom_fusion.27
  321.1 4.0 scatter_custom_fusion.28
  326.1 75.0 %psum.50 = f32[2,1]{0,1:T(1,128)S(1)} all-reduce(f32[2,1]{0,1:T(1,128)S(1)} %bitcast.877), channel_id=1, replica_groups=mesh['sub'=64,'slab'=4] {'sub','slab'}, use_global_device_ids=true, to_apply=%region_34.35 | all-reduce | flops 2 | bytes 16 | tf_op jit(solution)/shard_map/psum | solution.py:236
  401.7 74.1 %psum.51 = f32[2]{0:T(128)S(1)} all-reduce(f32[2]{0:T(128)S(1)} %reduce_sum.129), channel_id=1, replica_groups=mesh['sub'=64,'slab'=4] {'sub','slab'}, use_global_device_ids=true, to_apply=%region_37.38 | all-reduce | flops 2 | bytes 16 | tf_op jit(solution)/shard_map/psum | solution.py:156
  502.8 4.2 scatter_custom_fusion.32
  507.0 4.0 scatter_custom_fusion.33
  525.9 4.0 pad_add_fusion.3
  540.7 4.3 collective-permute-start.33
  554.8 4.0 scatter_custom_fusion.37
  558.9 4.4 scatter_custom_fusion.38
  582.0 4.0 pad_add_fusion.2
  596.0 4.3 collective-permute-start.38
  611.1 4.0 scatter_custom_fusion.42
  615.2 4.0 scatter_custom_fusion.43
  620.4 74.9 %psum.52 = f32[2,2]{0,1:T(2,128)S(1)} all-reduce(f32[2,2]{0,1:T(2,128)S(1)} %pad_maximum_fusion.8), channel_id=1, replica_groups=mesh['sub'=64,'slab'=4] {'sub','slab'}, use_global_device_ids=true, to_apply=%region_57.58 | all-reduce | flops 4 | bytes 32 | tf_op jit(solution)/shard_map/psum | solution.py:236
  696.2 74.0 %psum.53 = f32[2]{0:T(128)S(1)} all-reduce(f32[2]{0:T(128)S(1)} %reduce_sum.144), channel_id=1, replica_groups=mesh['sub'=64,'slab'=4] {'sub','slab'}, use_global_device_ids=true, to_apply=%region_60.61 | all-reduce | flops 2 | bytes 16 | tf_op jit(solution)/shard_map/psum | solution.py:156
  800.4 4.4 scatter_custom_fusion.47
  804.8 4.0 scatter_custom_fusion.48
  823.7 4.1 pad_add_fusion.1
  837.8 4.3 collective-permute-start.48
  853.3 4.0 scatter_custom_fusion.52
  857.4 4.3 scatter_custom_fusion.53
  880.4 4.0 pad_add_fusion
  898.0 4.3 collective-permute-start.53
  914.9 4.0 scatter_custom_fusion.57
  919.0 4.0 scatter_custom_fusion.58
  924.5 74.4 %psum.54 = f32[2,3]{0,1:T(4,128)S(1)} all-reduce(f32[2,3]{0,1:T(4,128)S(1)} %pad_maximum_fusion.7), channel_id=1, replica_groups=mesh['sub'=64,'slab'=4] {'sub','slab'}, use_global_device_ids=true, to_apply=%region_83.84 | all-reduce | flops 6 | bytes 48 | tf_op jit(solution)/shard_map/psum | solution.py:236
  1003.1 74.3 %psum.55 = f32[2]{0:T(128)S(1)} all-reduce(f32[2]{0:T(128)S(1)} %reduce_sum.189), channel_id=1, replica_groups=mesh['sub'=64,'slab'=4] {'sub','slab'}, use_global_device_ids=true, to_apply=%region_86.87 | all-reduce | flops 2 | bytes 16 | tf_op jit(solution)/shard_map/psum | solution.py:156
  (1010 shorter events, 387.1 us)
Async XLA Ops:
  17.0 17.1 %collective-permute-start.2 = (f32[11,256]{0,1:T(8,128)S(1)}, f32[11,256]{0,1:T(8,128)S(1)}, u32[]{:S(2)}, u32[]{:S(2)}) collective-permute-start(f32[11,256]{0,1:T(8,128)S(1)} %multiply_bitcast_fusion.27), channel_id=1, source_target_pairs={{0,16},{16,0},{4,20},{20,4},{8,24},{24,8},{12,28},{28,12},{32,48},... | collective-permute-start | bytes 33800 | tf_op jit(solution)/shard_map/ppermute | solution.py:27
  21.8 12.4 %collective-permute-start.1 = (f32[11,256]{0,1:T(8,128)S(1)}, f32[11,256]{0,1:T(8,128)S(1)}, u32[]{:S(2)}, u32[]{:S(2)}) collective-permute-start(f32[11,256]{0,1:T(8,128)S(1)} %multiply_bitcast_fusion.28), channel_id=1, source_target_pairs={{0,8},{8,0},{4,12},{12,4},{16,24},{24,16},{20,28},{28,20},{32,40},... | collective-permute-start | bytes 33800 | tf_op jit(solution)/shard_map/ppermute | solution.py:27
  27.3 15.4 %collective-permute-start.3 = (f32[1,11,512]{1,2,0:T(8,128)}, f32[1,11,512]{1,2,0:T(8,128)S(1)}, u32[]{:S(2)}, u32[]{:S(2)}) collective-permute-start(f32[1,11,512]{1,2,0:T(8,128)} %bitcast.30), channel_id=1, source_target_pairs={{0,1},{1,2},{2,3},{4,5},{5,6},{6,7},{8,9},{9,10},{10,11},{12,13},{... | collective-permute-start | bytes 67592 | tf_op jit(solution)/shard_map/ppermute | solution.py:35
  31.6 15.1 %collective-permute-start.4 = (f32[1,11,512]{1,2,0:T(8,128)S(1)}, f32[1,11,512]{1,2,0:T(8,128)S(1)}, u32[]{:S(2)}, u32[]{:S(2)}) collective-permute-start(f32[1,11,512]{1,2,0:T(8,128)S(1)} %bitcast.841), channel_id=1, source_target_pairs={{1,0},{2,1},{3,2},{5,4},{6,5},{7,6},{9,8},{10,9},{11,10},{13,12},{... | collective-permute-start | bytes 67592 | tf_op jit(solution)/shard_map/ppermute | solution.py:38
  172.3 18.5 %collective-permute-start.7 = (f32[2,256]{0,1:T(8,128)S(1)}, f32[2,256]{0,1:T(8,128)S(1)}, u32[]{:S(2)}, u32[]{:S(2)}) collective-permute-start(f32[2,256]{0,1:T(8,128)S(1)} %multiply_bitcast_fusion.24), channel_id=1, source_target_pairs={{0,16},{16,0},{4,20},{20,4},{8,24},{24,8},{12,28},{28,12},{32,48},... | collective-permute-start | bytes 6152 | tf_op jit(solution)/shard_map/ppermute | solution.py:27
  177.6 17.3 %collective-permute-start.6 = (f32[2,256]{0,1:T(8,128)S(1)}, f32[2,256]{0,1:T(8,128)S(1)}, u32[]{:S(2)}, u32[]{:S(2)}) collective-permute-start(f32[2,256]{0,1:T(8,128)S(1)} %multiply_bitcast_fusion.25), channel_id=1, source_target_pairs={{0,8},{8,0},{4,12},{12,4},{16,24},{24,16},{20,28},{28,20},{32,40},... | collective-permute-start | bytes 6152 | tf_op jit(solution)/shard_map/ppermute | solution.py:27
  181.1 15.1 %collective-permute-start.5 = (f32[2,256]{0,1:T(8,128)S(1)}, f32[2,256]{0,1:T(8,128)S(1)}, u32[]{:S(2)}, u32[]{:S(2)}) collective-permute-start(f32[2,256]{0,1:T(8,128)S(1)} %multiply_bitcast_fusion.26), channel_id=1, source_target_pairs={{0,4},{4,0},{8,12},{12,8},{16,20},{20,16},{24,28},{28,24},{32,36},... | collective-permute-start | bytes 6152 | tf_op jit(solution)/shard_map/ppermute | solution.py:27
  182.2 29.1 %collective-permute-start.8 = (f32[1,2,512]{1,2,0:T(8,128)}, f32[1,2,512]{1,2,0:T(8,128)S(1)}, u32[]{:S(2)}, u32[]{:S(2)}) collective-permute-start(f32[1,2,512]{1,2,0:T(8,128)} %bitcast.54), channel_id=1, source_target_pairs={{0,1},{1,2},{2,3},{4,5},{5,6},{6,7},{8,9},{9,10},{10,11},{12,13},{... | collective-permute-start | bytes 12296 | tf_op jit(solution)/shard_map/ppermute | solution.py:35
  183.5 31.9 %collective-permute-start.9 = (f32[1,2,512]{1,2,0:T(8,128)}, f32[1,2,512]{1,2,0:T(8,128)S(1)}, u32[]{:S(2)}, u32[]{:S(2)}) collective-permute-start(f32[1,2,512]{1,2,0:T(8,128)} %bitcast.878), channel_id=1, source_target_pairs={{1,0},{2,1},{3,2},{5,4},{6,5},{7,6},{9,8},{10,9},{11,10},{13,12},{... | collective-permute-start | bytes 12296 | tf_op jit(solution)/shard_map/ppermute | solution.py:38
  190.8 13.7 %collective-permute-start.13 = (f32[1,1,512]{2,1,0:T(1,128)S(1)}, f32[1,1,512]{2,1,0:T(1,128)S(1)}, u32[]{:S(2)}, u32[]{:S(2)}) collective-permute-start(f32[1,1,512]{2,1,0:T(1,128)S(1)} %bitcast.865), channel_id=1, source_target_pairs={{0,1},{1,2},{2,3},{4,5},{5,6},{6,7},{8,9},{9,10},{10,11},{12,13},{... | collective-permute-start | bytes 6152 | tf_op jit(solution)/shard_map/ppermute | solution.py:35
  194.9 13.0 %collective-permute-start.14 = (f32[1,1,512]{2,1,0:T(1,128)S(1)}, f32[1,1,512]{2,1,0:T(1,128)S(1)}, u32[]{:S(2)}, u32[]{:S(2)}) collective-permute-start(f32[1,1,512]{2,1,0:T(1,128)S(1)} %bitcast.864), channel_id=1, source_target_pairs={{1,0},{2,1},{3,2},{5,4},{6,5},{7,6},{9,8},{10,9},{11,10},{13,12},{... | collective-permute-start | bytes 6152 | tf_op jit(solution)/shard_map/ppermute | solution.py:38
  240.9 12.2 %collective-permute-start.17 = (f32[6,256]{0,1:T(8,128)S(1)}, f32[6,256]{0,1:T(8,128)S(1)}, u32[]{:S(2)}, u32[]{:S(2)}) collective-permute-start(f32[6,256]{0,1:T(8,128)S(1)} %multiply_bitcast_fusion.21), channel_id=1, source_target_pairs={{0,16},{16,0},{4,20},{20,4},{8,24},{24,8},{12,28},{28,12},{32,48},... | collective-permute-start | bytes 18440 | tf_op jit(solution)/shard_map/ppermute | solution.py:27
  241.1 12.1 %collective-permute-start.16 = (f32[6,256]{0,1:T(8,128)S(1)}, f32[6,256]{0,1:T(8,128)S(1)}, u32[]{:S(2)}, u32[]{:S(2)}) collective-permute-start(f32[6,256]{0,1:T(8,128)S(1)} %multiply_bitcast_fusion.22), channel_id=1, source_target_pairs={{0,8},{8,0},{4,12},{12,4},{16,24},{24,16},{20,28},{28,20},{32,40},... | collective-permute-start | bytes 18440 | tf_op jit(solution)/shard_map/ppermute | solution.py:27
  242.5 10.9 %collective-permute-start.15 = (f32[6,256]{0,1:T(8,128)S(1)}, f32[6,256]{0,1:T(8,128)S(1)}, u32[]{:S(2)}, u32[]{:S(2)}) collective-permute-start(f32[6,256]{0,1:T(8,128)S(1)} %multiply_bitcast_fusion.23), channel_id=1, source_target_pairs={{0,4},{4,0},{8,12},{12,8},{16,20},{20,16},{24,28},{28,24},{32,36},... | collective-permute-start | bytes 18440 | tf_op jit(solution)/shard_map/ppermute | solution.py:27
  247.5 14.0 %collective-permute-start.18 = (f32[1,6,512]{1,2,0:T(8,128)}, f32[1,6,512]{1,2,0:T(8,128)S(1)}, u32[]{:S(2)}, u32[]{:S(2)}) collective-permute-start(f32[1,6,512]{1,2,0:T(8,128)} %bitcast.96), channel_id=1, source_target_pairs={{0,1},{1,2},{2,3},{4,5},{5,6},{6,7},{8,9},{9,10},{10,11},{12,13},{... | collective-permute-start | bytes 36872 | tf_op jit(solution)/shard_map/ppermute | solution.py:35
  251.8 13.8 %collective-permute-start.19 = (f32[1,6,512]{1,2,0:T(8,128)}, f32[1,6,512]{1,2,0:T(8,128)S(1)}, u32[]{:S(2)}, u32[]{:S(2)}) collective-permute-start(f32[1,6,512]{1,2,0:T(8,128)} %bitcast.867), channel_id=1, source_target_pairs={{1,0},{2,1},{3,2},{5,4},{6,5},{7,6},{9,8},{10,9},{11,10},{13,12},{... | collective-permute-start | bytes 36872 | tf_op jit(solution)/shard_map/ppermute | solution.py:38
  295.5 13.0 %collective-permute-start.22 = (f32[8,256]{0,1:T(8,128)S(1)}, f32[8,256]{0,1:T(8,128)S(1)}, u32[]{:S(2)}, u32[]{:S(2)}) collective-permute-start(f32[8,256]{0,1:T(8,128)S(1)} %multiply_bitcast_fusion.18), channel_id=1, source_target_pairs={{0,16},{16,0},{4,20},{20,4},{8,24},{24,8},{12,28},{28,12},{32,48},... | collective-permute-start | bytes 24584 | tf_op jit(solution)/shard_map/ppermute | solution.py:27
  296.6 12.0 %collective-permute-start.21 = (f32[8,256]{0,1:T(8,128)S(1)}, f32[8,256]{0,1:T(8,128)S(1)}, u32[]{:S(2)}, u32[]{:S(2)}) collective-permute-start(f32[8,256]{0,1:T(8,128)S(1)} %multiply_bitcast_fusion.19), channel_id=1, source_target_pairs={{0,8},{8,0},{4,12},{12,4},{16,24},{24,16},{20,28},{28,20},{32,40},... | collective-permute-start | bytes 24584 | tf_op jit(solution)/shard_map/ppermute | solution.py:27
  302.9 14.1 %collective-permute-start.23 = (f32[1,8,512]{1,2,0:T(8,128)}, f32[1,8,512]{1,2,0:T(8,128)S(1)}, u32[]{:S(2)}, u32[]{:S(2)}) collective-permute-start(f32[1,8,512]{1,2,0:T(8,128)} %bitcast.125), channel_id=1, source_target_pairs={{0,1},{1,2},{2,3},{4,5},{5,6},{6,7},{8,9},{9,10},{10,11},{12,13},{... | collective-permute-start | bytes 49160 | tf_op jit(solution)/shard_map/ppermute | solution.py:35
  307.2 13.9 %collective-permute-start.24 = (f32[1,8,512]{1,2,0:T(8,128)}, f32[1,8,512]{1,2,0:T(8,128)S(1)}, u32[]{:S(2)}, u32[]{:S(2)}) collective-permute-start(f32[1,8,512]{1,2,0:T(8,128)} %bitcast.870), channel_id=1, source_target_pairs={{1,0},{2,1},{3,2},{5,4},{6,5},{7,6},{9,8},{10,9},{11,10},{13,12},{... | collective-permute-start | bytes 49160 | tf_op jit(solution)/shard_map/ppermute | solution.py:38
  483.4 10.9 %collective-permute-start.27 = (f32[2,256]{0,1:T(8,128)S(1)}, f32[2,256]{0,1:T(8,128)S(1)}, u32[]{:S(2)}, u32[]{:S(2)}) collective-permute-start(f32[2,256]{0,1:T(8,128)S(1)} %multiply_bitcast_fusion.15), channel_id=1, source_target_pairs={{0,16},{16,0},{4,20},{20,4},{8,24},{24,8},{12,28},{28,12},{32,48},... | collective-permute-start | bytes 6152 | tf_op jit(solution)/shard_map/ppermute | solution.py:27
  483.6 10.8 collective-permute-start.26
  490.4 12.3 %collective-permute-start.28 = (f32[1,2,512]{1,2,0:T(8,128)}, f32[1,2,512]{1,2,0:T(8,128)S(1)}, u32[]{:S(2)}, u32[]{:S(2)}) collective-permute-start(f32[1,2,512]{1,2,0:T(8,128)} %bitcast.152), channel_id=1, source_target_pairs={{0,1},{1,2},{2,3},{4,5},{5,6},{6,7},{8,9},{9,10},{10,11},{12,13},{... | collective-permute-start | bytes 12296 | tf_op jit(solution)/shard_map/ppermute | solution.py:35
  493.0 14.0 %collective-permute-start.29 = (f32[1,2,512]{1,2,0:T(8,128)}, f32[1,2,512]{1,2,0:T(8,128)S(1)}, u32[]{:S(2)}, u32[]{:S(2)}) collective-permute-start(f32[1,2,512]{1,2,0:T(8,128)} %bitcast.880), channel_id=1, source_target_pairs={{1,0},{2,1},{3,2},{5,4},{6,5},{7,6},{9,8},{10,9},{11,10},{13,12},{... | collective-permute-start | bytes 12296 | tf_op jit(solution)/shard_map/ppermute | solution.py:38
  532.8 13.6 %collective-permute-start.32 = (f32[6,256]{0,1:T(8,128)S(1)}, f32[6,256]{0,1:T(8,128)S(1)}, u32[]{:S(2)}, u32[]{:S(2)}) collective-permute-start(f32[6,256]{0,1:T(8,128)S(1)} %multiply_bitcast_fusion.12), channel_id=1, source_target_pairs={{0,16},{16,0},{4,20},{20,4},{8,24},{24,8},{12,28},{28,12},{32,48},... | collective-permute-start | bytes 18440 | tf_op jit(solution)/shard_map/ppermute | solution.py:27
  534.9 11.5 %collective-permute-start.31 = (f32[6,256]{0,1:T(8,128)S(1)}, f32[6,256]{0,1:T(8,128)S(1)}, u32[]{:S(2)}, u32[]{:S(2)}) collective-permute-start(f32[6,256]{0,1:T(8,128)S(1)} %multiply_bitcast_fusion.13), channel_id=1, source_target_pairs={{0,8},{8,0},{4,12},{12,4},{16,24},{24,16},{20,28},{28,20},{32,40},... | collective-permute-start | bytes 18440 | tf_op jit(solution)/shard_map/ppermute | solution.py:27
  536.4 10.1 collective-permute-start.30
  540.7 14.1 %collective-permute-start.33 = (f32[1,6,512]{1,2,0:T(8,128)}, f32[1,6,512]{1,2,0:T(8,128)S(1)}, u32[]{:S(2)}, u32[]{:S(2)}) collective-permute-start(f32[1,6,512]{1,2,0:T(8,128)} %bitcast.177), channel_id=1, source_target_pairs={{0,1},{1,2},{2,3},{4,5},{5,6},{6,7},{8,9},{9,10},{10,11},{12,13},{... | collective-permute-start | bytes 36872 | tf_op jit(solution)/shard_map/ppermute | solution.py:35
  545.0 13.8 %collective-permute-start.34 = (f32[1,6,512]{1,2,0:T(8,128)}, f32[1,6,512]{1,2,0:T(8,128)S(1)}, u32[]{:S(2)}, u32[]{:S(2)}) collective-permute-start(f32[1,6,512]{1,2,0:T(8,128)} %bitcast.868), channel_id=1, source_target_pairs={{1,0},{2,1},{3,2},{5,4},{6,5},{7,6},{9,8},{10,9},{11,10},{13,12},{... | collective-permute-start | bytes 36872 | tf_op jit(solution)/shard_map/ppermute | solution.py:38
  588.9 12.8 %collective-permute-start.37 = (f32[8,256]{0,1:T(8,128)S(1)}, f32[8,256]{0,1:T(8,128)S(1)}, u32[]{:S(2)}, u32[]{:S(2)}) collective-permute-start(f32[8,256]{0,1:T(8,128)S(1)} %multiply_bitcast_fusion.9), channel_id=1, source_target_pairs={{0,16},{16,0},{4,20},{20,4},{8,24},{24,8},{12,28},{28,12},{32,48},... | collective-permute-start | bytes 24584 | tf_op jit(solution)/shard_map/ppermute | solution.py:27
  589.1 12.6 %collective-permute-start.36 = (f32[8,256]{0,1:T(8,128)S(1)}, f32[8,256]{0,1:T(8,128)}, u32[]{:S(2)}, u32[]{:S(2)}) collective-permute-start(f32[8,256]{0,1:T(8,128)S(1)} %multiply_bitcast_fusion.10), channel_id=1, source_target_pairs={{0,8},{8,0},{4,12},{12,4},{16,24},{24,16},{20,28},{28,20},{32,40},... | collective-permute-start | bytes 24584 | tf_op jit(solution)/shard_map/ppermute | solution.py:27
  591.1 11.6 %collective-permute-start.35 = (f32[8,256]{0,1:T(8,128)}, f32[8,256]{0,1:T(8,128)S(1)}, u32[]{:S(2)}, u32[]{:S(2)}) collective-permute-start(f32[8,256]{0,1:T(8,128)} %multiply_bitcast_fusion.11), channel_id=1, source_target_pairs={{0,4},{4,0},{8,12},{12,8},{16,20},{20,16},{24,28},{28,24},{32,36},... | collective-permute-start | bytes 24584 | tf_op jit(solution)/shard_map/ppermute | solution.py:27
  596.0 15.0 %collective-permute-start.38 = (f32[1,8,512]{1,2,0:T(8,128)}, f32[1,8,512]{1,2,0:T(8,128)S(1)}, u32[]{:S(2)}, u32[]{:S(2)}) collective-permute-start(f32[1,8,512]{1,2,0:T(8,128)} %bitcast.203), channel_id=1, source_target_pairs={{0,1},{1,2},{2,3},{4,5},{5,6},{6,7},{8,9},{9,10},{10,11},{12,13},{... | collective-permute-start | bytes 49160 | tf_op jit(solution)/shard_map/ppermute | solution.py:35
  600.3 14.8 %collective-permute-start.39 = (f32[1,8,512]{1,2,0:T(8,128)}, f32[1,8,512]{1,2,0:T(8,128)S(1)}, u32[]{:S(2)}, u32[]{:S(2)}) collective-permute-start(f32[1,8,512]{1,2,0:T(8,128)} %bitcast.871), channel_id=1, source_target_pairs={{1,0},{2,1},{3,2},{5,4},{6,5},{7,6},{9,8},{10,9},{11,10},{13,12},{... | collective-permute-start | bytes 49160 | tf_op jit(solution)/shard_map/ppermute | solution.py:38
  777.8 13.6 %collective-permute-start.42 = (f32[2,256]{0,1:T(8,128)S(1)}, f32[2,256]{0,1:T(8,128)S(1)}, u32[]{:S(2)}, u32[]{:S(2)}) collective-permute-start(f32[2,256]{0,1:T(8,128)S(1)} %multiply_bitcast_fusion.6), channel_id=1, source_target_pairs={{0,16},{16,0},{4,20},{20,4},{8,24},{24,8},{12,28},{28,12},{32,48},... | collective-permute-start | bytes 6152 | tf_op jit(solution)/shard_map/ppermute | solution.py:27
  779.1 12.3 %collective-permute-start.41 = (f32[2,256]{0,1:T(8,128)}, f32[2,256]{0,1:T(8,128)S(1)}, u32[]{:S(2)}, u32[]{:S(2)}) collective-permute-start(f32[2,256]{0,1:T(8,128)} %multiply_bitcast_fusion.7), channel_id=1, source_target_pairs={{0,8},{8,0},{4,12},{12,4},{16,24},{24,16},{20,28},{28,20},{32,40},... | collective-permute-start | bytes 6152 | tf_op jit(solution)/shard_map/ppermute | solution.py:27
  787.0 13.3 %collective-permute-start.43 = (f32[1,2,512]{1,2,0:T(8,128)}, f32[1,2,512]{1,2,0:T(8,128)S(1)}, u32[]{:S(2)}, u32[]{:S(2)}) collective-permute-start(f32[1,2,512]{1,2,0:T(8,128)} %bitcast.234), channel_id=1, source_target_pairs={{0,1},{1,2},{2,3},{4,5},{5,6},{6,7},{8,9},{9,10},{10,11},{12,13},{... | collective-permute-start | bytes 12296 | tf_op jit(solution)/shard_map/ppermute | solution.py:35
  790.0 14.8 %collective-permute-start.44 = (f32[1,2,512]{1,2,0:T(8,128)}, f32[1,2,512]{1,2,0:T(8,128)S(1)}, u32[]{:S(2)}, u32[]{:S(2)}) collective-permute-start(f32[1,2,512]{1,2,0:T(8,128)} %bitcast.879), channel_id=1, source_target_pairs={{1,0},{2,1},{3,2},{5,4},{6,5},{7,6},{9,8},{10,9},{11,10},{13,12},{... | collective-permute-start | bytes 12296 | tf_op jit(solution)/shard_map/ppermute | solution.py:38
  830.7 13.3 %collective-permute-start.47 = (f32[6,256]{0,1:T(8,128)S(1)}, f32[6,256]{0,1:T(8,128)S(1)}, u32[]{:S(2)}, u32[]{:S(2)}) collective-permute-start(f32[6,256]{0,1:T(8,128)S(1)} %multiply_bitcast_fusion.3), channel_id=1, source_target_pairs={{0,16},{16,0},{4,20},{20,4},{8,24},{24,8},{12,28},{28,12},{32,48},... | collective-permute-start | bytes 18440 | tf_op jit(solution)/shard_map/ppermute | solution.py:27
  832.1 11.9 %collective-permute-start.46 = (f32[6,256]{0,1:T(8,128)S(1)}, f32[6,256]{0,1:T(8,128)S(1)}, u32[]{:S(2)}, u32[]{:S(2)}) collective-permute-start(f32[6,256]{0,1:T(8,128)S(1)} %multiply_bitcast_fusion.4), channel_id=1, source_target_pairs={{0,8},{8,0},{4,12},{12,4},{16,24},{24,16},{20,28},{28,20},{32,40},... | collective-permute-start | bytes 18440 | tf_op jit(solution)/shard_map/ppermute | solution.py:27
  833.0 11.2 %collective-permute-start.45 = (f32[6,256]{0,1:T(8,128)}, f32[6,256]{0,1:T(8,128)}, u32[]{:S(2)}, u32[]{:S(2)}) collective-permute-start(f32[6,256]{0,1:T(8,128)} %multiply_bitcast_fusion.5), channel_id=1, source_target_pairs={{0,4},{4,0},{8,12},{12,8},{16,20},{20,16},{24,28},{28,24},{32,36},... | collective-permute-start | bytes 18440 | tf_op jit(solution)/shard_map/ppermute | solution.py:27
  837.8 15.6 %collective-permute-start.48 = (f32[1,6,512]{1,2,0:T(8,128)}, f32[1,6,512]{1,2,0:T(8,128)S(1)}, u32[]{:S(2)}, u32[]{:S(2)}) collective-permute-start(f32[1,6,512]{1,2,0:T(8,128)} %bitcast.258), channel_id=1, source_target_pairs={{0,1},{1,2},{2,3},{4,5},{5,6},{6,7},{8,9},{9,10},{10,11},{12,13},{... | collective-permute-start | bytes 36872 | tf_op jit(solution)/shard_map/ppermute | solution.py:35
  842.1 15.3 %collective-permute-start.49 = (f32[1,6,512]{1,2,0:T(8,128)}, f32[1,6,512]{1,2,0:T(8,128)S(1)}, u32[]{:S(2)}, u32[]{:S(2)}) collective-permute-start(f32[1,6,512]{1,2,0:T(8,128)} %bitcast.869), channel_id=1, source_target_pairs={{1,0},{2,1},{3,2},{5,4},{6,5},{7,6},{9,8},{10,9},{11,10},{13,12},{... | collective-permute-start | bytes 36872 | tf_op jit(solution)/shard_map/ppermute | solution.py:38
  887.2 16.7 %collective-permute-start.52 = (f32[8,256]{0,1:T(8,128)S(1)}, f32[8,256]{0,1:T(8,128)}, u32[]{:S(2)}, u32[]{:S(2)}) collective-permute-start(f32[8,256]{0,1:T(8,128)S(1)} %multiply_bitcast_fusion), channel_id=1, source_target_pairs={{0,16},{16,0},{4,20},{20,4},{8,24},{24,8},{12,28},{28,12},{32,48},... | collective-permute-start | bytes 24584 | tf_op jit(solution)/shard_map/ppermute | solution.py:27
  888.9 15.9 %collective-permute-start.51 = (f32[8,256]{0,1:T(8,128)}, f32[8,256]{0,1:T(8,128)}, u32[]{:S(2)}, u32[]{:S(2)}) collective-permute-start(f32[8,256]{0,1:T(8,128)} %multiply_bitcast_fusion.1), channel_id=1, source_target_pairs={{0,8},{8,0},{4,12},{12,4},{16,24},{24,16},{20,28},{28,20},{32,40},... | collective-permute-start | bytes 24584 | tf_op jit(solution)/shard_map/ppermute | solution.py:27
  891.4 14.5 %collective-permute-start.50 = (f32[8,256]{0,1:T(8,128)}, f32[8,256]{0,1:T(8,128)}, u32[]{:S(2)}, u32[]{:S(2)}) collective-permute-start(f32[8,256]{0,1:T(8,128)} %multiply_bitcast_fusion.2), channel_id=1, source_target_pairs={{0,4},{4,0},{8,12},{12,8},{16,20},{20,16},{24,28},{28,24},{32,36},... | collective-permute-start | bytes 24584 | tf_op jit(solution)/shard_map/ppermute | solution.py:27
  898.0 16.9 %collective-permute-start.53 = (f32[1,8,512]{1,2,0:T(8,128)}, f32[1,8,512]{1,2,0:T(8,128)S(1)}, u32[]{:S(2)}, u32[]{:S(2)}) collective-permute-start(f32[1,8,512]{1,2,0:T(8,128)} %bitcast.284), channel_id=1, source_target_pairs={{0,1},{1,2},{2,3},{4,5},{5,6},{6,7},{8,9},{9,10},{10,11},{12,13},{... | collective-permute-start | bytes 49160 | tf_op jit(solution)/shard_map/ppermute | solution.py:35
  902.3 16.7 %collective-permute-start.54 = (f32[1,8,512]{1,2,0:T(8,128)}, f32[1,8,512]{1,2,0:T(8,128)S(1)}, u32[]{:S(2)}, u32[]{:S(2)}) collective-permute-start(f32[1,8,512]{1,2,0:T(8,128)} %bitcast.866), channel_id=1, source_target_pairs={{1,0},{2,1},{3,2},{5,4},{6,5},{7,6},{9,8},{10,9},{11,10},{13,12},{... | collective-permute-start | bytes 49160 | tf_op jit(solution)/shard_map/ppermute | solution.py:38
  (119 other events, 2818.9 us)
where the time goes:
time: 1090 us; the launch traced here: 1080 us
  blocking collectives  526 us (48%)
  other arithmetic  226 us (21%)
  local copies, waits for them, and re-layouts  218 us (20%)
  starting transfers between devices  93.7 us (9%)
    psum x4, blocking collectives, weighted_norms(): lax.psum(jnp.sum(weights * vectors * vectors, axis=(1, 2)), ('sub', 'slab'))  301 us
    psum x3, blocking collectives, per_device(): heights = lax.psum(local_heights, ('sub', 'slab'))  224 us
    scatter-add x33, other arithmetic, assemble(): summed = summed.at[:, iface_nodes[matching]].add(incoming[matching])  82.6 us
    another operation x136, local copies, waits for them, and re-layouts, node_sums(): corner_block = element_out[:, corner].reshape(channels, EX, EY, EZ)  72.7 us
    scatter-add x11, other arithmetic, assemble(): return summed.at[:, face_nodes[1]].add(extended[3])  44.3 us
    scatter-add x11, other arithmetic, assemble(): summed = summed.at[:, face_nodes[0]].add(extended[0])  44.3 us
    ppermute x11, starting transfers between devices, extended_2(): lax.ppermute(lax.slice_in_dim(block, block.shape[dim] - width, None, axis...  39.7 us
    ppermute x33, starting transfers between devices, swapped(): return lax.ppermute(block, axis, route)  39.5 us
  transfers between devices with their start and end apart: 55, of which 1 were waited for; matrix products, arithmetic and copies ran while one was open for 17% of the time, Pallas kernels for 0%

commit v1 on v0

--- a/solution.py
+++ b/solution.py
@@ -153,7 +153,7 @@
 
 
 def weighted_norms(vectors, weights):
-    return lax.psum(jnp.sum(weights * vectors * vectors, axis=(1, 2)), ("sub", "slab"))
+    return lax.psum(lax.psum(jnp.sum(weights * vectors * vectors, axis=(1, 2)), "sub"), "slab")
 
 
 def triangular_solves(factor, target):

time: 1090 us -> 1330 us (1.22)
  blocking collectives: 526 us -> 756 us
    psum x4 -> x8, blocking collectives: 301 us -> 531 us  [the longest x4 496 us: weighted_norms(): lax.psum(jnp.sum(weights * vectors * vectors, axis=(1, 2)), 'sub')]
  transfers between devices with their start and end apart: 55 -> 55, of which waited for: 1 -> 0; matrix products, arithmetic and copies ran while one was open for 17% -> 14% of each run, Pallas kernels for 0% -> 0%
where the time goes in v1:
time: 1330 us; the launch traced here: 1320 us
  blocking collectives  756 us (57%)
  other arithmetic  226 us (17%)
  local copies, waits for them, and re-layouts  217 us (16%)
  starting transfers between devices  100 us (8%)
    psum x4, blocking collectives, weighted_norms(): lax.psum(jnp.sum(weights * vectors * vectors, axis=(1, 2)), 'sub')  496 us
    psum x3, blocking collectives, per_device(): heights = lax.psum(local_heights, ('sub', 'slab'))  226 us
    scatter-add x33, other arithmetic, assemble(): summed = summed.at[:, iface_nodes[matching]].add(incoming[matching])  83 us
    another operation x136, local copies, waits for them, and re-layouts, node_sums(): corner_block = element_out[:, corner].reshape(channels, EX, EY, EZ)  72.7 us
    ppermute x33, starting transfers between devices, swapped(): return lax.ppermute(block, axis, route)  46.1 us
    scatter-add x11, other arithmetic, assemble(): return summed.at[:, face_nodes[1]].add(extended[3])  44.9 us
    scatter-add x11, other arithmetic, assemble(): summed = summed.at[:, face_nodes[0]].add(extended[0])  43.7 us
    ppermute x11, starting transfers between devices, extended_2(): lax.ppermute(lax.slice_in_dim(block, block.shape[dim] - width, None, axis...  39.7 us
  transfers between devices with their start and end apart: 55, of which 0 were waited for; matrix products, arithmetic and copies ran while one was open for 14% of the time, Pallas kernels for 0%

profile of v1, /device:TPU:1, one launch (start us, length us, event | category | flops | bytes accessed | tf_op | source)
XLA Modules:
  0.0 1315.5 jit_solution(14887674441806735688)
XLA Ops:
  17.0 3.9 collective-permute-start.2
  42.8 3.9 scatter_custom_fusion.7
  46.8 3.9 scatter_custom_fusion.8
  51.5 124.1 %psum.77 = f32[2]{0:T(128)S(1)} all-reduce(f32[2]{0:T(128)S(1)} %reduce_sum.120), channel_id=1, replica_groups=mesh['sub'=64,'slab'=4] {'sub'}, use_global_device_ids=true, to_apply=%region_11.12 | all-reduce | flops 2 | bytes 16 | tf_op jit(solution)/shard_map/psum | solution.py:156
  176.1 10.2 psum.78
  230.2 7.7 collective-permute-start.10
  249.3 4.0 collective-permute-start.13
  266.4 3.3 scatter_fusion.10
  269.8 4.1 scatter_custom_fusion.12
  273.9 3.9 scatter_custom_fusion.13
  292.7 4.0 pad_add_fusion.5
  306.0 4.3 collective-permute-start.18
  320.0 4.0 scatter_custom_fusion.22
  324.1 4.2 scatter_custom_fusion.23
  347.0 4.0 pad_add_fusion.4
  362.2 4.3 collective-permute-start.23
  376.3 4.0 scatter_custom_fusion.27
  380.4 4.0 scatter_custom_fusion.28
  385.3 74.4 %psum.79 = f32[2,1]{0,1:T(1,128)S(1)} all-reduce(f32[2,1]{0,1:T(1,128)S(1)} %bitcast.878), channel_id=1, replica_groups=mesh['sub'=64,'slab'=4] {'sub','slab'}, use_global_device_ids=true, to_apply=%region_35.36 | all-reduce | flops 2 | bytes 16 | tf_op jit(solution)/shard_map/psum | solution.py:236
  460.3 124.1 %psum.80 = f32[2]{0:T(128)S(1)} all-reduce(f32[2]{0:T(128)S(1)} %reduce_sum.129), channel_id=1, replica_groups=mesh['sub'=64,'slab'=4] {'sub'}, use_global_device_ids=true, to_apply=%region_38.39 | all-reduce | flops 2 | bytes 16 | tf_op jit(solution)/shard_map/psum | solution.py:156
  584.5 7.6 psum.81
  600.7 4.1 collective-permute-start.25
  620.9 4.0 scatter_custom_fusion.32
  625.0 4.2 scatter_custom_fusion.33
  644.0 4.0 pad_add_fusion.3
  660.4 4.3 collective-permute-start.33
  674.7 4.0 scatter_custom_fusion.37
  678.8 4.4 scatter_custom_fusion.38
  701.9 4.0 pad_add_fusion.2
  714.2 4.3 collective-permute-start.38
  729.3 4.0 scatter_custom_fusion.42
  733.4 4.0 scatter_custom_fusion.43
  738.6 75.6 %psum.82 = f32[2,2]{0,1:T(2,128)S(1)} all-reduce(f32[2,2]{0,1:T(2,128)S(1)} %pad_maximum_fusion.8), channel_id=1, replica_groups=mesh['sub'=64,'slab'=4] {'sub','slab'}, use_global_device_ids=true, to_apply=%region_59.60 | all-reduce | flops 4 | bytes 32 | tf_op jit(solution)/shard_map/psum | solution.py:236
  815.4 124.1 %psum.83 = f32[2]{0:T(128)S(1)} all-reduce(f32[2]{0:T(128)S(1)} %reduce_sum.144), channel_id=1, replica_groups=mesh['sub'=64,'slab'=4] {'sub'}, use_global_device_ids=true, to_apply=%region_62.63 | all-reduce | flops 2 | bytes 16 | tf_op jit(solution)/shard_map/psum | solution.py:156
  939.5 8.3 psum.84
  976.5 4.0 scatter_custom_fusion.47
  980.6 4.4 scatter_custom_fusion.48
  999.9 4.1 pad_add_fusion.1
  1016.9 4.3 collective-permute-start.48
  1032.6 4.0 scatter_custom_fusion.52
  1036.7 4.3 scatter_custom_fusion.53
  1059.7 4.0 pad_add_fusion
  1074.1 4.3 collective-permute-start.53
  1090.1 4.0 scatter_custom_fusion.57
  1094.2 4.0 scatter_custom_fusion.58
  1099.7 75.6 %psum.85 = f32[2,3]{0,1:T(4,128)S(1)} all-reduce(f32[2,3]{0,1:T(4,128)S(1)} %pad_maximum_fusion.7), channel_id=1, replica_groups=mesh['sub'=64,'slab'=4] {'sub','slab'}, use_global_device_ids=true, to_apply=%region_86.87 | all-reduce | flops 6 | bytes 48 | tf_op jit(solution)/shard_map/psum | solution.py:236
  1176.3 124.1 %psum.86 = f32[2]{0:T(128)S(1)} all-reduce(f32[2]{0:T(128)S(1)} %reduce_sum.189), channel_id=1, replica_groups=mesh['sub'=64,'slab'=4] {'sub'}, use_global_device_ids=true, to_apply=%region_89.90 | all-reduce | flops 2 | bytes 16 | tf_op jit(solution)/shard_map/psum | solution.py:156
  1303.6 8.1 psum.87
  (1014 shorter events, 398.6 us)
Async XLA Ops:
  17.0 17.1 %collective-permute-start.2 = (f32[11,256]{0,1:T(8,128)S(1)}, f32[11,256]{0,1:T(8,128)S(1)}, u32[]{:S(2)}, u32[]{:S(2)}) collective-permute-start(f32[11,256]{0,1:T(8,128)S(1)} %multiply_bitcast_fusion.27), channel_id=1, source_target_pairs={{0,16},{16,0},{4,20},{20,4},{8,24},{24,8},{12,28},{28,12},{32,48},... | collective-permute-start | bytes 33800 | tf_op jit(solution)/shard_map/ppermute | solution.py:27
  21.8 12.4 collective-permute-start.1
  27.3 15.4 %collective-permute-start.3 = (f32[1,11,512]{1,2,0:T(8,128)}, f32[1,11,512]{1,2,0:T(8,128)S(1)}, u32[]{:S(2)}, u32[]{:S(2)}) collective-permute-start(f32[1,11,512]{1,2,0:T(8,128)} %bitcast.30), channel_id=1, source_target_pairs={{0,1},{1,2},{2,3},{4,5},{5,6},{6,7},{8,9},{9,10},{10,11},{12,13},{... | collective-permute-start | bytes 67592 | tf_op jit(solution)/shard_map/ppermute | solution.py:35
  31.6 15.1 %collective-permute-start.4 = (f32[1,11,512]{1,2,0:T(8,128)S(1)}, f32[1,11,512]{1,2,0:T(8,128)S(1)}, u32[]{:S(2)}, u32[]{:S(2)}) collective-permute-start(f32[1,11,512]{1,2,0:T(8,128)S(1)} %bitcast.842), channel_id=1, source_target_pairs={{1,0},{2,1},{3,2},{5,4},{6,5},{7,6},{9,8},{10,9},{11,10},{13,12},{... | collective-permute-start | bytes 67592 | tf_op jit(solution)/shard_map/ppermute | solution.py:38
  227.5 21.8 %collective-permute-start.7 = (f32[2,256]{0,1:T(8,128)S(1)}, f32[2,256]{0,1:T(8,128)S(1)}, u32[]{:S(2)}, u32[]{:S(2)}) collective-permute-start(f32[2,256]{0,1:T(8,128)S(1)} %multiply_bitcast_fusion.24), channel_id=1, source_target_pairs={{0,16},{16,0},{4,20},{20,4},{8,24},{24,8},{12,28},{28,12},{32,48},... | collective-permute-start | bytes 6152 | tf_op jit(solution)/shard_map/ppermute | solution.py:27
  227.8 12.2 collective-permute-start.12
  230.2 11.8 collective-permute-start.10
  238.0 15.4 %collective-permute-start.6 = (f32[2,256]{0,1:T(8,128)S(1)}, f32[2,256]{0,1:T(8,128)S(1)}, u32[]{:S(2)}, u32[]{:S(2)}) collective-permute-start(f32[2,256]{0,1:T(8,128)S(1)} %multiply_bitcast_fusion.25), channel_id=1, source_target_pairs={{0,8},{8,0},{4,12},{12,4},{16,24},{24,16},{20,28},{28,20},{32,40},... | collective-permute-start | bytes 6152 | tf_op jit(solution)/shard_map/ppermute | solution.py:27
  240.0 14.7 %collective-permute-start.5 = (f32[2,256]{0,1:T(8,128)S(1)}, f32[2,256]{0,1:T(8,128)S(1)}, u32[]{:S(2)}, u32[]{:S(2)}) collective-permute-start(f32[2,256]{0,1:T(8,128)S(1)} %multiply_bitcast_fusion.26), channel_id=1, source_target_pairs={{0,4},{4,0},{8,12},{12,8},{16,20},{20,16},{24,28},{28,24},{32,36},... | collective-permute-start | bytes 6152 | tf_op jit(solution)/shard_map/ppermute | solution.py:27
  240.7 29.1 %collective-permute-start.8 = (f32[1,2,512]{1,2,0:T(8,128)}, f32[1,2,512]{1,2,0:T(8,128)S(1)}, u32[]{:S(2)}, u32[]{:S(2)}) collective-permute-start(f32[1,2,512]{1,2,0:T(8,128)} %bitcast.54), channel_id=1, source_target_pairs={{0,1},{1,2},{2,3},{4,5},{5,6},{6,7},{8,9},{9,10},{10,11},{12,13},{... | collective-permute-start | bytes 12296 | tf_op jit(solution)/shard_map/ppermute | solution.py:35
  242.0 31.9 %collective-permute-start.9 = (f32[1,2,512]{1,2,0:T(8,128)}, f32[1,2,512]{1,2,0:T(8,128)S(1)}, u32[]{:S(2)}, u32[]{:S(2)}) collective-permute-start(f32[1,2,512]{1,2,0:T(8,128)} %bitcast.879), channel_id=1, source_target_pairs={{1,0},{2,1},{3,2},{5,4},{6,5},{7,6},{9,8},{10,9},{11,10},{13,12},{... | collective-permute-start | bytes 12296 | tf_op jit(solution)/shard_map/ppermute | solution.py:38
  249.3 13.7 %collective-permute-start.13 = (f32[1,1,512]{2,1,0:T(1,128)S(1)}, f32[1,1,512]{2,1,0:T(1,128)S(1)}, u32[]{:S(2)}, u32[]{:S(2)}) collective-permute-start(f32[1,1,512]{2,1,0:T(1,128)S(1)} %bitcast.866), channel_id=1, source_target_pairs={{0,1},{1,2},{2,3},{4,5},{5,6},{6,7},{8,9},{9,10},{10,11},{12,13},{... | collective-permute-start | bytes 6152 | tf_op jit(solution)/shard_map/ppermute | solution.py:35
  253.4 13.0 collective-permute-start.14
  299.4 12.2 collective-permute-start.17
  306.0 14.0 %collective-permute-start.18 = (f32[1,6,512]{1,2,0:T(8,128)}, f32[1,6,512]{1,2,0:T(8,128)S(1)}, u32[]{:S(2)}, u32[]{:S(2)}) collective-permute-start(f32[1,6,512]{1,2,0:T(8,128)} %bitcast.96), channel_id=1, source_target_pairs={{0,1},{1,2},{2,3},{4,5},{5,6},{6,7},{8,9},{9,10},{10,11},{12,13},{... | collective-permute-start | bytes 36872 | tf_op jit(solution)/shard_map/ppermute | solution.py:35
  310.3 13.8 %collective-permute-start.19 = (f32[1,6,512]{1,2,0:T(8,128)}, f32[1,6,512]{1,2,0:T(8,128)S(1)}, u32[]{:S(2)}, u32[]{:S(2)}) collective-permute-start(f32[1,6,512]{1,2,0:T(8,128)} %bitcast.868), channel_id=1, source_target_pairs={{1,0},{2,1},{3,2},{5,4},{6,5},{7,6},{9,8},{10,9},{11,10},{13,12},{... | collective-permute-start | bytes 36872 | tf_op jit(solution)/shard_map/ppermute | solution.py:38
  353.9 13.8 %collective-permute-start.22 = (f32[8,256]{0,1:T(8,128)S(1)}, f32[8,256]{0,1:T(8,128)S(1)}, u32[]{:S(2)}, u32[]{:S(2)}) collective-permute-start(f32[8,256]{0,1:T(8,128)S(1)} %multiply_bitcast_fusion.18), channel_id=1, source_target_pairs={{0,16},{16,0},{4,20},{20,4},{8,24},{24,8},{12,28},{28,12},{32,48},... | collective-permute-start | bytes 24584 | tf_op jit(solution)/shard_map/ppermute | solution.py:27
  355.9 11.9 collective-permute-start.21
  362.2 14.1 %collective-permute-start.23 = (f32[1,8,512]{1,2,0:T(8,128)}, f32[1,8,512]{1,2,0:T(8,128)S(1)}, u32[]{:S(2)}, u32[]{:S(2)}) collective-permute-start(f32[1,8,512]{1,2,0:T(8,128)} %bitcast.125), channel_id=1, source_target_pairs={{0,1},{1,2},{2,3},{4,5},{5,6},{6,7},{8,9},{9,10},{10,11},{12,13},{... | collective-permute-start | bytes 49160 | tf_op jit(solution)/shard_map/ppermute | solution.py:35
  366.4 13.9 %collective-permute-start.24 = (f32[1,8,512]{1,2,0:T(8,128)}, f32[1,8,512]{1,2,0:T(8,128)S(1)}, u32[]{:S(2)}, u32[]{:S(2)}) collective-permute-start(f32[1,8,512]{1,2,0:T(8,128)} %bitcast.871), channel_id=1, source_target_pairs={{1,0},{2,1},{3,2},{5,4},{6,5},{7,6},{9,8},{10,9},{11,10},{13,12},{... | collective-permute-start | bytes 49160 | tf_op jit(solution)/shard_map/ppermute | solution.py:38
  599.6 12.9 collective-permute-start.27
  599.8 12.7 collective-permute-start.26
  600.7 12.0 collective-permute-start.25
  608.1 12.8 collective-permute-start.28
  611.2 13.8 %collective-permute-start.29 = (f32[1,2,512]{1,2,0:T(8,128)}, f32[1,2,512]{1,2,0:T(8,128)S(1)}, u32[]{:S(2)}, u32[]{:S(2)}) collective-permute-start(f32[1,2,512]{1,2,0:T(8,128)} %bitcast.881), channel_id=1, source_target_pairs={{1,0},{2,1},{3,2},{5,4},{6,5},{7,6},{9,8},{10,9},{11,10},{13,12},{... | collective-permute-start | bytes 12296 | tf_op jit(solution)/shard_map/ppermute | solution.py:38
  650.9 15.1 %collective-permute-start.32 = (f32[6,256]{0,1:T(8,128)S(1)}, f32[6,256]{0,1:T(8,128)S(1)}, u32[]{:S(2)}, u32[]{:S(2)}) collective-permute-start(f32[6,256]{0,1:T(8,128)S(1)} %multiply_bitcast_fusion.12), channel_id=1, source_target_pairs={{0,16},{16,0},{4,20},{20,4},{8,24},{24,8},{12,28},{28,12},{32,48},... | collective-permute-start | bytes 18440 | tf_op jit(solution)/shard_map/ppermute | solution.py:27
  653.8 12.4 collective-permute-start.31
  660.4 14.3 %collective-permute-start.33 = (f32[1,6,512]{1,2,0:T(8,128)}, f32[1,6,512]{1,2,0:T(8,128)S(1)}, u32[]{:S(2)}, u32[]{:S(2)}) collective-permute-start(f32[1,6,512]{1,2,0:T(8,128)} %bitcast.177), channel_id=1, source_target_pairs={{0,1},{1,2},{2,3},{4,5},{5,6},{6,7},{8,9},{9,10},{10,11},{12,13},{... | collective-permute-start | bytes 36872 | tf_op jit(solution)/shard_map/ppermute | solution.py:35
  664.7 14.1 %collective-permute-start.34 = (f32[1,6,512]{1,2,0:T(8,128)}, f32[1,6,512]{1,2,0:T(8,128)S(1)}, u32[]{:S(2)}, u32[]{:S(2)}) collective-permute-start(f32[1,6,512]{1,2,0:T(8,128)} %bitcast.869), channel_id=1, source_target_pairs={{1,0},{2,1},{3,2},{5,4},{6,5},{7,6},{9,8},{10,9},{11,10},{13,12},{... | collective-permute-start | bytes 36872 | tf_op jit(solution)/shard_map/ppermute | solution.py:38
  708.8 11.0 collective-permute-start.37
  709.0 10.9 collective-permute-start.36
  709.9 11.0 collective-permute-start.35
  714.2 15.0 %collective-permute-start.38 = (f32[1,8,512]{1,2,0:T(8,128)}, f32[1,8,512]{1,2,0:T(8,128)S(1)}, u32[]{:S(2)}, u32[]{:S(2)}) collective-permute-start(f32[1,8,512]{1,2,0:T(8,128)} %bitcast.203), channel_id=1, source_target_pairs={{0,1},{1,2},{2,3},{4,5},{5,6},{6,7},{8,9},{9,10},{10,11},{12,13},{... | collective-permute-start | bytes 49160 | tf_op jit(solution)/shard_map/ppermute | solution.py:35
  718.5 14.8 %collective-permute-start.39 = (f32[1,8,512]{1,2,0:T(8,128)}, f32[1,8,512]{1,2,0:T(8,128)S(1)}, u32[]{:S(2)}, u32[]{:S(2)}) collective-permute-start(f32[1,8,512]{1,2,0:T(8,128)} %bitcast.872), channel_id=1, source_target_pairs={{1,0},{2,1},{3,2},{5,4},{6,5},{7,6},{9,8},{10,9},{11,10},{13,12},{... | collective-permute-start | bytes 49160 | tf_op jit(solution)/shard_map/ppermute | solution.py:38
  955.4 12.1 collective-permute-start.42
  956.3 11.3 collective-permute-start.41
  963.6 12.9 collective-permute-start.43
  966.2 14.4 %collective-permute-start.44 = (f32[1,2,512]{1,2,0:T(8,128)}, f32[1,2,512]{1,2,0:T(8,128)S(1)}, u32[]{:S(2)}, u32[]{:S(2)}) collective-permute-start(f32[1,2,512]{1,2,0:T(8,128)} %bitcast.880), channel_id=1, source_target_pairs={{1,0},{2,1},{3,2},{5,4},{6,5},{7,6},{9,8},{10,9},{11,10},{13,12},{... | collective-permute-start | bytes 12296 | tf_op jit(solution)/shard_map/ppermute | solution.py:38
  1006.8 16.3 %collective-permute-start.47 = (f32[6,256]{0,1:T(8,128)S(1)}, f32[6,256]{0,1:T(8,128)S(1)}, u32[]{:S(2)}, u32[]{:S(2)}) collective-permute-start(f32[6,256]{0,1:T(8,128)S(1)} %multiply_bitcast_fusion.3), channel_id=1, source_target_pairs={{0,16},{16,0},{4,20},{20,4},{8,24},{24,8},{12,28},{28,12},{32,48},... | collective-permute-start | bytes 18440 | tf_op jit(solution)/shard_map/ppermute | solution.py:27
  1009.6 13.6 %collective-permute-start.46 = (f32[6,256]{0,1:T(8,128)S(1)}, f32[6,256]{0,1:T(8,128)S(1)}, u32[]{:S(2)}, u32[]{:S(2)}) collective-permute-start(f32[6,256]{0,1:T(8,128)S(1)} %multiply_bitcast_fusion.4), channel_id=1, source_target_pairs={{0,8},{8,0},{4,12},{12,4},{16,24},{24,16},{20,28},{28,20},{32,40},... | collective-permute-start | bytes 18440 | tf_op jit(solution)/shard_map/ppermute | solution.py:27
  1012.2 11.1 collective-permute-start.45
  1016.9 15.7 %collective-permute-start.48 = (f32[1,6,512]{1,2,0:T(8,128)}, f32[1,6,512]{1,2,0:T(8,128)S(1)}, u32[]{:S(2)}, u32[]{:S(2)}) collective-permute-start(f32[1,6,512]{1,2,0:T(8,128)} %bitcast.258), channel_id=1, source_target_pairs={{0,1},{1,2},{2,3},{4,5},{5,6},{6,7},{8,9},{9,10},{10,11},{12,13},{... | collective-permute-start | bytes 36872 | tf_op jit(solution)/shard_map/ppermute | solution.py:35
  1021.2 15.5 %collective-permute-start.49 = (f32[1,6,512]{1,2,0:T(8,128)}, f32[1,6,512]{1,2,0:T(8,128)S(1)}, u32[]{:S(2)}, u32[]{:S(2)}) collective-permute-start(f32[1,6,512]{1,2,0:T(8,128)} %bitcast.870), channel_id=1, source_target_pairs={{1,0},{2,1},{3,2},{5,4},{6,5},{7,6},{9,8},{10,9},{11,10},{13,12},{... | collective-permute-start | bytes 36872 | tf_op jit(solution)/shard_map/ppermute | solution.py:38
  1066.5 13.5 %collective-permute-start.52 = (f32[8,256]{0,1:T(8,128)S(1)}, f32[8,256]{0,1:T(8,128)S(1)}, u32[]{:S(2)}, u32[]{:S(2)}) collective-permute-start(f32[8,256]{0,1:T(8,128)S(1)} %multiply_bitcast_fusion), channel_id=1, source_target_pairs={{0,16},{16,0},{4,20},{20,4},{8,24},{24,8},{12,28},{28,12},{32,48},... | collective-permute-start | bytes 24584 | tf_op jit(solution)/shard_map/ppermute | solution.py:27
  1067.3 12.7 collective-permute-start.51
  1068.1 12.9 collective-permute-start.50
  1074.1 16.0 %collective-permute-start.53 = (f32[1,8,512]{1,2,0:T(8,128)}, f32[1,8,512]{1,2,0:T(8,128)S(1)}, u32[]{:S(2)}, u32[]{:S(2)}) collective-permute-start(f32[1,8,512]{1,2,0:T(8,128)} %bitcast.284), channel_id=1, source_target_pairs={{0,1},{1,2},{2,3},{4,5},{5,6},{6,7},{8,9},{9,10},{10,11},{12,13},{... | collective-permute-start | bytes 49160 | tf_op jit(solution)/shard_map/ppermute | solution.py:35
  1078.4 15.8 %collective-permute-start.54 = (f32[1,8,512]{1,2,0:T(8,128)}, f32[1,8,512]{1,2,0:T(8,128)S(1)}, u32[]{:S(2)}, u32[]{:S(2)}) collective-permute-start(f32[1,8,512]{1,2,0:T(8,128)} %bitcast.867), channel_id=1, source_target_pairs={{1,0},{2,1},{3,2},{5,4},{6,5},{7,6},{9,8},{10,9},{11,10},{13,12},{... | collective-permute-start | bytes 49160 | tf_op jit(solution)/shard_map/ppermute | solution.py:38
  (119 other events, 3340.9 us)
